TPU v7x, 256 devices: a whole 4x4x8 slice. The times are simulated.
256 devices in a mesh: row: 4 (over y), col: 16 (over z, core), layer: 4 (over x).
Axes of the slice: x: 4, y: 4, z: 8, core: 2. Of those that a mesh axis runs over, the one named last changes fastest.
Arguments:
- blocks: bfloat16 [5632, 128, 128], P(('col', 'layer')), may hold values from -6 to 6
- block_aux: int32 [5632], P(('col', 'layer')), may hold values from 0 to 23
- block_row: int32 [5632], P(('col', 'layer')), may hold values from 0 to 15, as said below
- block_col: int32 [5632], P(('col', 'layer')), may hold values from 0 to 159, as said below
- extents: int32 [5632], P(('col', 'layer')), may hold values from 32 to 128
- occ_green: bfloat16 [20480, 2048], P('layer', 'row'), may hold values from -0.00390625 to 0.00390625
- virt_green: bfloat16 [20480, 2048], P('layer', 'row'), may hold values from -0.00390625 to 0.00390625
Outputs:
- chi: float32 [24, 24], replicated
Inputs may be any that keep to these rules, and one draw needn't show every extreme that they name: block_row[n] numbers the block of 128 window functions that tile n covers. The owner of tile n is the pair (block_row[n], block_col[n] // 40). Within each device's share of 88 consecutive entries no owner appears more than 2 times, and one owner, the same for every share, appears exactly 2 times in every share.
All inputs are finite; a program needn't handle non-finite values.
Results may differ from a plain program's by a relative error of at most 0.0003.
Values may be sent and summed in bfloat16 or wider, within the bound.
No kernel may reach another device: no remote copies, remote signals or barrier semaphores. Data moves between devices by JAX's collectives and lax.ppermute only.
A program may use at most 192 MiB of HBM per device.

v0:
```python
import jax
import jax.numpy as jnp
from jax import lax
from jax.sharding import PartitionSpec as P

NP = 24


def on_device(blocks, block_aux, block_row, block_col, extents, occ_green, virt_green):
    row_count = lax.axis_size("row")
    col_count = lax.axis_size("col")
    layer_count = lax.axis_size("layer")
    held_count = blocks.shape[0]
    tile_side = blocks.shape[1]
    aux_count = NP
    owner_count = col_count * layer_count
    capacity = max(2, held_count // owner_count + 1)
    layer_blocks = occ_green.shape[0] // tile_side
    columns = jnp.arange(tile_side, dtype=jnp.int32)
    masked_tiles = jnp.where(
        columns[None, None, :] < extents[:, None, None], blocks, jnp.zeros((), blocks.dtype)
    )
    layer_of = block_col // layer_blocks
    target = block_row * layer_count + layer_of
    kept_col = block_col - layer_of * layer_blocks
    marked = (target[:, None] == jnp.arange(owner_count, dtype=jnp.int32)[None, :]).astype(
        jnp.int32
    )
    earlier = jnp.cumsum(marked, axis=0) - marked
    placed = target * capacity + jnp.sum(earlier * marked, axis=1)
    send_tiles = (
        jnp.zeros((owner_count * capacity, tile_side, tile_side), blocks.dtype)
        .at[placed]
        .set(masked_tiles)
    )
    send_meta = (
        jnp.zeros((owner_count * capacity, 2), jnp.int32)
        .at[placed]
        .set(jnp.stack([block_aux, kept_col], axis=1))
    )
    send_tiles = send_tiles.reshape(col_count, layer_count, capacity, tile_side, tile_side)
    send_meta = send_meta.reshape(col_count, layer_count, capacity, 2)
    total_slots = col_count * layer_count * capacity
    got_tiles, got_meta = (
        lax.all_to_all(
            send_tiles.reshape(total_slots, tile_side, tile_side),
            ("col", "layer"),
            split_axis=0,
            concat_axis=0,
            tiled=True,
        ),
        lax.all_to_all(
            send_meta.reshape(total_slots, 2),
            ("col", "layer"),
            split_axis=0,
            concat_axis=0,
            tiled=True,
        ),
    )
    group_size = col_count * capacity
    got_tiles = got_tiles.reshape(layer_count, group_size, tile_side, tile_side)
    got_meta = got_meta.reshape(layer_count, group_size, 2)
    occ_cols, virt_cols = (occ_green, virt_green)
    width_here = occ_cols.shape[1]
    offsets = jnp.arange(tile_side, dtype=jnp.int32)

    def add_group(totals, record):
        occ_total, virt_total = totals
        tile_group, meta_group = record
        row_index = meta_group[:, 1][:, None] * tile_side + offsets[None, :]
        occ_rows = occ_cols[row_index]
        virt_rows = virt_cols[row_index]
        occ_term = jnp.einsum(
            "gsv,gls->gvl", occ_rows, tile_group, preferred_element_type=jnp.float32
        )
        virt_term = jnp.einsum(
            "gvs,gsl->gvl", tile_group, virt_rows, preferred_element_type=jnp.float32
        )
        aux_index = meta_group[:, 0]
        return (
            (occ_total.at[aux_index].add(occ_term), virt_total.at[aux_index].add(virt_term)),
            None,
        )

    start_totals = (
        jnp.zeros((aux_count, width_here, tile_side), jnp.float32),
        jnp.zeros((aux_count, tile_side, width_here), jnp.float32),
    )
    (occ_total, virt_total), _ = lax.scan(add_group, start_totals, (got_tiles, got_meta))
    occ_done, virt_done = (
        lax.psum_scatter(occ_total, "layer", scatter_dimension=1, tiled=True),
        lax.psum_scatter(virt_total, "layer", scatter_dimension=2, tiled=True),
    )
    mesh_count = row_count * layer_count
    thin_rows = tile_side // mesh_count
    stack_count = mesh_count // col_count
    narrow = occ_done.shape[1]
    occ_five = occ_done.reshape(aux_count, 1, col_count, thin_rows, tile_side)
    virt_five = virt_done.reshape(aux_count, stack_count, col_count, thin_rows, narrow)
    occ_moved, virt_moved = (
        lax.all_to_all(occ_five, "col", split_axis=2, concat_axis=1, tiled=True),
        lax.all_to_all(virt_five, "col", split_axis=2, concat_axis=1, tiled=True),
    )
    virt_four = virt_moved.reshape(aux_count, mesh_count, thin_rows, narrow)
    virt_back = lax.all_to_all(virt_four, ("row", "layer"), split_axis=1, concat_axis=3, tiled=True)
    occ_final = occ_moved.reshape(aux_count, col_count, thin_rows, tile_side)
    virt_final = virt_back.reshape(aux_count, thin_rows, col_count, tile_side)
    chi_part = jnp.einsum(
        "pcji,qjci->pq",
        occ_final,
        virt_final,
        precision=lax.Precision.HIGHEST,
        preferred_element_type=jnp.float32,
    )
    return lax.psum(chi_part, ("row", "col", "layer"))


def solution(mesh):
    in_specs = (
        P(("col", "layer"), None, None),
        P(("col", "layer")),
        P(("col", "layer")),
        P(("col", "layer")),
        P(("col", "layer")),
        P("layer", "row"),
        P("layer", "row"),
    )
    out_specs = P()
    return jax.shard_map(
        on_device, mesh=mesh, in_specs=in_specs, out_specs=out_specs, check_vma=False
    )
```

profile of v0, /device:TPU:1, one launch (start us, length us, event | category | flops | bytes accessed | tf_op | source)
XLA Modules:
  0.0 813.1 jit_solution(16769600088540931036)
XLA Ops:
  6.5 0.7 subtract_bitcast_fusion
  7.2 0.7 multiply_add_fusion
  7.9 0.1 fusion.21
  8.0 0.1 reduce_window_sum.11
  8.1 0.2 select_reduce_fusion
  8.3 0.7 pad_add_fusion
  8.9 0.1 copy.18
  9.0 0.8 scatter_custom_fusion.2
  9.9 1.1 copy.19
  11.0 13.0 %all-to-all-start = ((s32[64,2,2]{1,2,0:T(2,128)}), s32[64,2,2]{1,2,0:T(2,128)S(1)}, u32[]{:S(2)}, u32[]{:S(2)}) async-start(s32[64,2,2]{1,2,0:T(2,128)} %copy.19), calls=%async_computation | async-start | bytes 131072 | tf_op jit(solution)/shard_map/all_to_all | solution.py:52
  24.0 0.7 iota_compare_fusion
  24.7 2.1 broadcast_select_fusion
  26.8 3.0 broadcast_in_dim.41
  29.7 12.7 %scatter_fusion.2 = bf16[128,128,128]{2,1,0:T(8,128)(2,1)} fusion(bf16[128,128,128]{2,1,0:T(8,128)(2,1)} %broadcast_in_dim.41, s32[88]{0:T(128)S(1)} %compare_select_fusion.2, bf16[88,128,128]{2,1,0:T(8,128)(2,1)S(1)} %broadcast_select_fusion), kind=kCustom, calls=%fused_computation.5 | custom fusion | bytes 8651104 | tf_op jit(solution)/shard_map/scatter | solution.py:34
  42.4 0.0 all-to-all-done
  42.4 10.4 %all-to-all-start.1 = ((bf16[128,128,128]{2,1,0:T(8,128)(2,1)}), bf16[128,128,128]{2,1,0:T(8,128)(2,1)}, u32[]{:S(2)}, u32[]{:S(2)}) async-start(bf16[128,128,128]{2,1,0:T(8,128)(2,1)} %scatter_fusion.2), calls=%async_computation.1 | async-start | bytes 8388608 | tf_op jit(solution)/shard_map/all_to_all | solution.py:45
  52.9 0.0 reduce-scatter.5.cloned.1.call-start
  52.9 0.1 reshape.109
  53.0 93.4 %all-to-all-done.1 = bf16[128,128,128]{2,1,0:T(8,128)(2,1)} async-done(((bf16[128,128,128]{2,1,0:T(8,128)(2,1)}), bf16[128,128,128]{2,1,0:T(8,128)(2,1)}, u32[]{:S(2)}, u32[]{:S(2)}) %all-to-all-start.1) | async-done | bytes 4194336 | tf_op jit(solution)/shard_map/all_to_all | solution.py:45
  146.4 3.4 broadcast_in_dim.22
  149.8 3.4 broadcast_in_dim.38
  153.2 366.1 %while.13 = (s32[]{:T(128)}, f32[24,512,128]{2,1,0:T(8,128)}, f32[24,128,512]{2,1,0:T(8,128)}, s32[4,32,2]{1,0,2:T(4,128)S(1)}, bf16[5120,512]{1,0:T(8,128)(2,1)...) while((s32[]{:T(128)}, f32[24,512,128]{2,1,0:T(8,128)}, ...), condition=%wide.region_7.8_spmd.clone, body=%wide.region_4.7_spmd.clone.sunk | while | flops 1077956736 | bytes 94423512 | solution.py:89
  153.2 0.1 fusion.37
  153.3 20.6 %gather_fusion.1 = bf16[4096,512]{1,0:T(8,128)(2,1)} fusion(bf16[5120,512]{1,0:T(8,128)(2,1)} %get-tuple-element.167, s32[4096]{0:T(1024)S(1)} %fusion.37), kind=kCustom, calls=%fused_computation.1.clone.clone.1 | custom fusion | bytes 8404992 | tf_op jit(solution)/shard_map/while/body/eval_jaxpr/gather | solution.py:72
  173.8 7.0 fusion.39
  180.8 18.0 %scatter_fusion.1 = f32[24,128,512]{2,1,0:T(8,128)} fusion(f32[24,128,512]{2,1,0:T(8,128)} %get-tuple-element.155, s32[32]{0:T(128)S(1)} %get-tuple-element.143, f32[32,128,512]{2,1,0:T(8,128)} %fusion.39), kind=kCustom, calls=%fused_computation.3.clone.clone.1 | custom fusion | flops 2097152 | bytes 25165952 | tf_op jit(solution)/shard_map/while/body/eval_jaxpr/scatter-add | solution.py:81
  198.8 20.6 %gather_fusion = bf16[4096,512]{1,0:T(8,128)(2,1)} fusion(bf16[5120,512]{1,0:T(8,128)(2,1)} %get-tuple-element.165, s32[4096]{0:T(1024)S(1)} %fusion.37), kind=kCustom, calls=%fused_computation.clone.clone.1 | custom fusion | bytes 8404992 | tf_op jit(solution)/shard_map/while/body/eval_jaxpr/gather | solution.py:71
  219.3 7.0 fusion.38
  226.4 17.8 %scatter_fusion = f32[24,512,128]{2,1,0:T(8,128)} fusion(f32[24,512,128]{2,1,0:T(8,128)} %get-tuple-element.154, s32[32]{0:T(128)S(1)} %get-tuple-element.143, f32[32,512,128]{2,1,0:T(8,128)} %fusion.38), kind=kCustom, calls=%fused_computation.2.clone.clone.1 | custom fusion | flops 2097152 | bytes 25165952 | tf_op jit(solution)/shard_map/while/body/eval_jaxpr/scatter-add | solution.py:81
  244.2 0.1 fusion.37
  244.3 20.6 %gather_fusion.1 = bf16[4096,512]{1,0:T(8,128)(2,1)} fusion(bf16[5120,512]{1,0:T(8,128)(2,1)} %get-tuple-element.167, s32[4096]{0:T(1024)S(1)} %fusion.37), kind=kCustom, calls=%fused_computation.1.clone.clone.1 | custom fusion | bytes 8404992 | tf_op jit(solution)/shard_map/while/body/eval_jaxpr/gather | solution.py:72
  264.9 7.0 fusion.39
  271.8 18.1 %scatter_fusion.1 = f32[24,128,512]{2,1,0:T(8,128)} fusion(f32[24,128,512]{2,1,0:T(8,128)} %get-tuple-element.155, s32[32]{0:T(128)S(1)} %get-tuple-element.143, f32[32,128,512]{2,1,0:T(8,128)} %fusion.39), kind=kCustom, calls=%fused_computation.3.clone.clone.1 | custom fusion | flops 2097152 | bytes 25165952 | tf_op jit(solution)/shard_map/while/body/eval_jaxpr/scatter-add | solution.py:81
  289.9 20.6 %gather_fusion = bf16[4096,512]{1,0:T(8,128)(2,1)} fusion(bf16[5120,512]{1,0:T(8,128)(2,1)} %get-tuple-element.165, s32[4096]{0:T(1024)S(1)} %fusion.37), kind=kCustom, calls=%fused_computation.clone.clone.1 | custom fusion | bytes 8404992 | tf_op jit(solution)/shard_map/while/body/eval_jaxpr/gather | solution.py:71
  310.5 7.0 fusion.38
  317.5 18.1 %scatter_fusion = f32[24,512,128]{2,1,0:T(8,128)} fusion(f32[24,512,128]{2,1,0:T(8,128)} %get-tuple-element.154, s32[32]{0:T(128)S(1)} %get-tuple-element.143, f32[32,512,128]{2,1,0:T(8,128)} %fusion.38), kind=kCustom, calls=%fused_computation.2.clone.clone.1 | custom fusion | flops 2097152 | bytes 25165952 | tf_op jit(solution)/shard_map/while/body/eval_jaxpr/scatter-add | solution.py:81
  335.6 0.1 fusion.37
  335.7 20.6 %gather_fusion.1 = bf16[4096,512]{1,0:T(8,128)(2,1)} fusion(bf16[5120,512]{1,0:T(8,128)(2,1)} %get-tuple-element.167, s32[4096]{0:T(1024)S(1)} %fusion.37), kind=kCustom, calls=%fused_computation.1.clone.clone.1 | custom fusion | bytes 8404992 | tf_op jit(solution)/shard_map/while/body/eval_jaxpr/gather | solution.py:72
  356.3 7.0 fusion.39
  363.3 18.5 %scatter_fusion.1 = f32[24,128,512]{2,1,0:T(8,128)} fusion(f32[24,128,512]{2,1,0:T(8,128)} %get-tuple-element.155, s32[32]{0:T(128)S(1)} %get-tuple-element.143, f32[32,128,512]{2,1,0:T(8,128)} %fusion.39), kind=kCustom, calls=%fused_computation.3.clone.clone.1 | custom fusion | flops 2097152 | bytes 25165952 | tf_op jit(solution)/shard_map/while/body/eval_jaxpr/scatter-add | solution.py:81
  381.7 20.6 %gather_fusion = bf16[4096,512]{1,0:T(8,128)(2,1)} fusion(bf16[5120,512]{1,0:T(8,128)(2,1)} %get-tuple-element.165, s32[4096]{0:T(1024)S(1)} %fusion.37), kind=kCustom, calls=%fused_computation.clone.clone.1 | custom fusion | bytes 8404992 | tf_op jit(solution)/shard_map/while/body/eval_jaxpr/gather | solution.py:71
  402.3 7.0 fusion.38
  409.3 18.4 %scatter_fusion = f32[24,512,128]{2,1,0:T(8,128)} fusion(f32[24,512,128]{2,1,0:T(8,128)} %get-tuple-element.154, s32[32]{0:T(128)S(1)} %get-tuple-element.143, f32[32,512,128]{2,1,0:T(8,128)} %fusion.38), kind=kCustom, calls=%fused_computation.2.clone.clone.1 | custom fusion | flops 2097152 | bytes 25165952 | tf_op jit(solution)/shard_map/while/body/eval_jaxpr/scatter-add | solution.py:81
  427.7 0.1 fusion.37
  427.8 20.6 %gather_fusion.1 = bf16[4096,512]{1,0:T(8,128)(2,1)} fusion(bf16[5120,512]{1,0:T(8,128)(2,1)} %get-tuple-element.167, s32[4096]{0:T(1024)S(1)} %fusion.37), kind=kCustom, calls=%fused_computation.1.clone.clone.1 | custom fusion | bytes 8404992 | tf_op jit(solution)/shard_map/while/body/eval_jaxpr/gather | solution.py:72
  448.4 7.0 fusion.39
  455.4 18.1 %scatter_fusion.1 = f32[24,128,512]{2,1,0:T(8,128)} fusion(f32[24,128,512]{2,1,0:T(8,128)} %get-tuple-element.155, s32[32]{0:T(128)S(1)} %get-tuple-element.143, f32[32,128,512]{2,1,0:T(8,128)} %fusion.39), kind=kCustom, calls=%fused_computation.3.clone.clone.1 | custom fusion | flops 2097152 | bytes 25165952 | tf_op jit(solution)/shard_map/while/body/eval_jaxpr/scatter-add | solution.py:81
  473.5 20.6 %gather_fusion = bf16[4096,512]{1,0:T(8,128)(2,1)} fusion(bf16[5120,512]{1,0:T(8,128)(2,1)} %get-tuple-element.165, s32[4096]{0:T(1024)S(1)} %fusion.37), kind=kCustom, calls=%fused_computation.clone.clone.1 | custom fusion | bytes 8404992 | tf_op jit(solution)/shard_map/while/body/eval_jaxpr/gather | solution.py:71
  494.1 7.0 fusion.38
  501.1 18.2 %scatter_fusion = f32[24,512,128]{2,1,0:T(8,128)} fusion(f32[24,512,128]{2,1,0:T(8,128)} %get-tuple-element.154, s32[32]{0:T(128)S(1)} %get-tuple-element.143, f32[32,512,128]{2,1,0:T(8,128)} %fusion.38), kind=kCustom, calls=%fused_computation.2.clone.clone.1 | custom fusion | flops 2097152 | bytes 25165952 | tf_op jit(solution)/shard_map/while/body/eval_jaxpr/scatter-add | solution.py:81
  519.2 0.0 reduce-scatter.5.cloned.1.call-update
  519.3 0.2 reduce-scatter.3.cloned.1.call-start
  519.5 0.5 reduce-scatter.3.cloned.1.call-update
  520.0 66.1 %reduce-scatter.5.cloned.1.call-done = f32[24,128,128]{2,1,0:T(8,128)} async-done(((f32[24,128,512]{2,1,0:T(8,128)}), f32[24,128,128]{2,1,0:T(8,128)}) %reduce-scatter.5.cloned.1.call-update) | async-done | bytes 1572880 | tf_op jit(solution)/shard_map/reduce_scatter | solution.py:92
  586.1 3.5 copy.23
  589.6 7.7 all-to-all-start.3
  597.2 57.7 %reduce-scatter.3.cloned.1.call-done = f32[24,128,128]{2,1,0:T(8,128)} async-done(((f32[24,512,128]{2,1,0:T(8,128)}), f32[24,128,128]{2,1,0:T(8,128)}) %reduce-scatter.3.cloned.1.call-update) | async-done | bytes 1572880 | tf_op jit(solution)/shard_map/reduce_scatter | solution.py:91
  654.9 2.3 copy.22
  657.3 0.0 all-to-all-done.3
  657.3 47.2 %all_to_all.47 = f32[24,1,16,8,128]{4,0,3,1,2:T(8,128)S(1)} all-to-all(f32[24,1,16,8,128]{4,0,3,1,2:T(8,128)S(1)} %bitcast.69), channel_id=1, replica_groups=mesh['row'=4,'col'=16,'layer'=4] {'col'}, dimensions={2} | all-to-all | bytes 3145728 | tf_op jit(solution)/shard_map/all_to_all | solution.py:101
  704.5 27.5 %all_to_all.48 = f32[24,16,8,128]{3,0,2,1:T(8,128)S(1)} all-to-all(f32[24,16,8,128]{3,0,2,1:T(8,128)S(1)} %bitcast.68), channel_id=1, replica_groups=mesh['row'=4,'col'=16,'layer'=4] {'row','layer'}, dimensions={1} | all-to-all | bytes 3145728 | tf_op jit(solution)/shard_map/all_to_all | solution.py:105
  732.0 1.6 fusion.16
  733.5 72.8 %psum.7 = f32[24,24]{1,0:T(8,128)} all-reduce(f32[24,24]{1,0:T(8,128)S(1)} %fusion.16), channel_id=1, replica_groups=mesh['row'=4,'col'=16,'layer'=4] {'row','col','layer'}, use_global_device_ids=true, to_apply=%region_10.11 | all-reduce | flops 576 | bytes 4608 | tf_op jit(solution)/shard_map/psum | solution.py:115
  (10 shorter events, 0.1 us)
Async XLA Ops:
  11.0 31.5 %all-to-all-start = ((s32[64,2,2]{1,2,0:T(2,128)}), s32[64,2,2]{1,2,0:T(2,128)S(1)}, u32[]{:S(2)}, u32[]{:S(2)}) async-start(s32[64,2,2]{1,2,0:T(2,128)} %copy.19), calls=%async_computation | async-start | bytes 131072 | tf_op jit(solution)/shard_map/all_to_all | solution.py:52
  42.4 103.9 %all-to-all-start.1 = ((bf16[128,128,128]{2,1,0:T(8,128)(2,1)}), bf16[128,128,128]{2,1,0:T(8,128)(2,1)}, u32[]{:S(2)}, u32[]{:S(2)}) async-start(bf16[128,128,128]{2,1,0:T(8,128)(2,1)} %scatter_fusion.2), calls=%async_computation.1 | async-start | bytes 8388608 | tf_op jit(solution)/shard_map/all_to_all | solution.py:45
  52.9 533.3 %reduce-scatter.5.cloned.1.call-start = ((), (), s32[]{:S(2)}) async-start(), calls=%async_computation.8 | async-start | bytes 7864320 | tf_op jit(solution)/shard_map/reduce_scatter | solution.py:92
  519.3 135.7 %reduce-scatter.3.cloned.1.call-start = ((), (), s32[]{:S(2)}) async-start(), calls=%async_computation.7 | async-start | bytes 7864320 | tf_op jit(solution)/shard_map/reduce_scatter | solution.py:91
  589.6 67.7 %all-to-all-start.3 = ((f32[24,1,16,8,128]{4,0,3,1,2:T(8,128)}), f32[24,1,16,8,128]{4,0,3,1,2:T(8,128)S(1)}, u32[]{:S(2)}, u32[]{:S(2)}) async-start(f32[24,1,16,8,128]{4,0,3,1,2:T(8,128)} %bitcast.6), calls=%async_computation.5 | async-start | bytes 3145728 | tf_op jit(solution)/shard_map/all_to_all | solution.py:102
Sparse Core Ops, SparseCore 0:
  519.4 66.6 reduce-scatter.4
  588.7 66.2 reduce-scatter.2
where the time goes:
time: 815 us; the launch traced here: 813 us
  waiting for transfers between devices  218 us (27%)
  local copies, waits for them, and re-layouts  195 us (24%)
  other arithmetic  151 us (19%)
  blocking collectives  147 us (18%)
  matrix products  57.5 us (7%)
  starting transfers between devices  31.3 us (4%)
  between operations  13.5 us (2%)
    all_to_all x1, waiting for transfers between devices, on_device(): lax.all_to_all(send_tiles.reshape(total_slots, tile_side, tile_side), ('c...  93.4 us
    gather x4, local copies, waits for them, and re-layouts, add_group(): virt_rows = virt_cols[row_index]  82.3 us
    gather x4, local copies, waits for them, and re-layouts, add_group(): occ_rows = occ_cols[row_index]  82.3 us
    psum x1, blocking collectives, on_device(): return lax.psum(chi_part, ('row', 'col', 'layer'))  72.8 us
    scatter-add x4, other arithmetic, add_group(): virt_total.at[aux_index].add(virt_term)  72.6 us
    scatter-add x4, other arithmetic, add_group(): occ_total.at[aux_index].add(occ_term)  72.5 us
    reduce_scatter x1, waiting for transfers between devices, on_device(): lax.psum_scatter(virt_total, 'layer', scatter_dimension=2, tiled=True)  66.1 us
    reduce_scatter x1, waiting for transfers between devices, on_device(): lax.psum_scatter(occ_total, 'layer', scatter_dimension=1, tiled=True)  57.7 us
  transfers between devices with their start and end apart: 5, of which 3 were waited for; matrix products, arithmetic and copies ran while one was open for 3% of the time, Pallas kernels for 0%

commit v1 on v0

--- a/solution.py
+++ b/solution.py
@@ -4,6 +4,11 @@
 from jax.sharding import PartitionSpec as P
 
 NP = 24
+
+
+def summed_here(shard, name):
+    shards = lax.all_gather(shard, name)
+    return jnp.sum(shards, axis=0)
 
 
 def on_device(blocks, block_aux, block_row, block_col, extents, occ_green, virt_green):
@@ -112,7 +117,7 @@
         precision=lax.Precision.HIGHEST,
         preferred_element_type=jnp.float32,
     )
-    return lax.psum(chi_part, ("row", "col", "layer"))
+    return summed_here(chi_part, ("row", "col", "layer"))
 
 
 def solution(mesh):

time: 815 us -> 872 us (1.070)
  blocking collectives: 147 us -> 204 us
    all_gather x0 -> x1, blocking collectives: none -> 129 us  [summed_here(): shards = lax.all_gather(shard, name)]
    psum x1 -> x0, blocking collectives: 72.8 us -> none  [on_device(): return lax.psum(chi_part, ('row', 'col', 'layer'))]
where the time goes in v1:
time: 872 us; the launch traced here: 871 us
  waiting for transfers between devices  218 us (25%)
  blocking collectives  204 us (23%)
  local copies, waits for them, and re-layouts  195 us (22%)
  other arithmetic  152 us (17%)
  matrix products  57.5 us (7%)
  starting transfers between devices  31.3 us (4%)
  between operations  13.5 us (2%)
    all_gather x1, blocking collectives, summed_here(): shards = lax.all_gather(shard, name)  129 us
    all_to_all x1, waiting for transfers between devices, on_device(): lax.all_to_all(send_tiles.reshape(total_slots, tile_side, tile_side), ('c...  93.4 us
    gather x4, local copies, waits for them, and re-layouts, add_group(): virt_rows = virt_cols[row_index]  82.3 us
    gather x4, local copies, waits for them, and re-layouts, add_group(): occ_rows = occ_cols[row_index]  82.3 us
    scatter-add x4, other arithmetic, add_group(): virt_total.at[aux_index].add(virt_term)  72.6 us
    scatter-add x4, other arithmetic, add_group(): occ_total.at[aux_index].add(occ_term)  72.5 us
    reduce_scatter x1, waiting for transfers between devices, on_device(): lax.psum_scatter(virt_total, 'layer', scatter_dimension=2, tiled=True)  66.1 us
    reduce_scatter x1, waiting for transfers between devices, on_device(): lax.psum_scatter(occ_total, 'layer', scatter_dimension=1, tiled=True)  57.7 us
  transfers between devices with their start and end apart: 5, of which 3 were waited for; matrix products, arithmetic and copies ran while one was open for 3% of the time, Pallas kernels for 0%

profile of v1, /device:TPU:1, one launch (start us, length us, event | category | flops | bytes accessed | tf_op | source)
XLA Modules:
  0.0 870.5 jit_solution(16094583937185909920)
XLA Ops:
  6.5 0.7 subtract_bitcast_fusion
  7.2 0.7 multiply_add_fusion
  7.9 0.1 fusion.21
  8.0 0.1 reduce_window_sum.11
  8.1 0.2 select_reduce_fusion
  8.3 0.7 pad_add_fusion
  8.9 0.1 copy.18
  9.0 0.8 scatter_custom_fusion.2
  9.9 1.1 copy.19
  11.0 13.0 %all-to-all-start = ((s32[64,2,2]{1,2,0:T(2,128)}), s32[64,2,2]{1,2,0:T(2,128)S(1)}, u32[]{:S(2)}, u32[]{:S(2)}) async-start(s32[64,2,2]{1,2,0:T(2,128)} %copy.19), calls=%async_computation | async-start | bytes 131072 | tf_op jit(solution)/shard_map/all_to_all | solution.py:57
  24.0 0.7 iota_compare_fusion
  24.7 2.1 broadcast_select_fusion
  26.8 3.0 broadcast_in_dim.41
  29.7 12.7 %scatter_fusion.2 = bf16[128,128,128]{2,1,0:T(8,128)(2,1)} fusion(bf16[128,128,128]{2,1,0:T(8,128)(2,1)} %broadcast_in_dim.41, s32[88]{0:T(128)S(1)} %compare_select_fusion.2, bf16[88,128,128]{2,1,0:T(8,128)(2,1)S(1)} %broadcast_select_fusion), kind=kCustom, calls=%fused_computation.5 | custom fusion | bytes 8651104 | tf_op jit(solution)/shard_map/scatter | solution.py:39
  42.4 0.0 all-to-all-done
  42.4 10.4 %all-to-all-start.1 = ((bf16[128,128,128]{2,1,0:T(8,128)(2,1)}), bf16[128,128,128]{2,1,0:T(8,128)(2,1)}, u32[]{:S(2)}, u32[]{:S(2)}) async-start(bf16[128,128,128]{2,1,0:T(8,128)(2,1)} %scatter_fusion.2), calls=%async_computation.1 | async-start | bytes 8388608 | tf_op jit(solution)/shard_map/all_to_all | solution.py:50
  52.9 0.0 reduce-scatter.5.cloned.1.call-start
  52.9 0.1 reshape.109
  53.0 93.4 %all-to-all-done.1 = bf16[128,128,128]{2,1,0:T(8,128)(2,1)} async-done(((bf16[128,128,128]{2,1,0:T(8,128)(2,1)}), bf16[128,128,128]{2,1,0:T(8,128)(2,1)}, u32[]{:S(2)}, u32[]{:S(2)}) %all-to-all-start.1) | async-done | bytes 4194336 | tf_op jit(solution)/shard_map/all_to_all | solution.py:50
  146.4 3.4 broadcast_in_dim.22
  149.8 3.4 broadcast_in_dim.38
  153.2 366.1 %while.13 = (s32[]{:T(128)}, f32[24,512,128]{2,1,0:T(8,128)}, f32[24,128,512]{2,1,0:T(8,128)}, s32[4,32,2]{1,0,2:T(4,128)S(1)}, bf16[5120,512]{1,0:T(8,128)(2,1)...) while((s32[]{:T(128)}, f32[24,512,128]{2,1,0:T(8,128)}, ...), condition=%wide.region_7.8_spmd.clone, body=%wide.region_4.7_spmd.clone.sunk | while | flops 1077956736 | bytes 94423512 | solution.py:94
  153.2 0.1 fusion.37
  153.3 20.6 %gather_fusion.1 = bf16[4096,512]{1,0:T(8,128)(2,1)} fusion(bf16[5120,512]{1,0:T(8,128)(2,1)} %get-tuple-element.167, s32[4096]{0:T(1024)S(1)} %fusion.37), kind=kCustom, calls=%fused_computation.1.clone.clone.1 | custom fusion | bytes 8404992 | tf_op jit(solution)/shard_map/while/body/eval_jaxpr/gather | solution.py:77
  173.8 7.0 fusion.39
  180.8 18.0 %scatter_fusion.1 = f32[24,128,512]{2,1,0:T(8,128)} fusion(f32[24,128,512]{2,1,0:T(8,128)} %get-tuple-element.155, s32[32]{0:T(128)S(1)} %get-tuple-element.143, f32[32,128,512]{2,1,0:T(8,128)} %fusion.39), kind=kCustom, calls=%fused_computation.3.clone.clone.1 | custom fusion | flops 2097152 | bytes 25165952 | tf_op jit(solution)/shard_map/while/body/eval_jaxpr/scatter-add | solution.py:86
  198.8 20.6 %gather_fusion = bf16[4096,512]{1,0:T(8,128)(2,1)} fusion(bf16[5120,512]{1,0:T(8,128)(2,1)} %get-tuple-element.165, s32[4096]{0:T(1024)S(1)} %fusion.37), kind=kCustom, calls=%fused_computation.clone.clone.1 | custom fusion | bytes 8404992 | tf_op jit(solution)/shard_map/while/body/eval_jaxpr/gather | solution.py:76
  219.3 7.0 fusion.38
  226.4 17.8 %scatter_fusion = f32[24,512,128]{2,1,0:T(8,128)} fusion(f32[24,512,128]{2,1,0:T(8,128)} %get-tuple-element.154, s32[32]{0:T(128)S(1)} %get-tuple-element.143, f32[32,512,128]{2,1,0:T(8,128)} %fusion.38), kind=kCustom, calls=%fused_computation.2.clone.clone.1 | custom fusion | flops 2097152 | bytes 25165952 | tf_op jit(solution)/shard_map/while/body/eval_jaxpr/scatter-add | solution.py:86
  244.2 0.1 fusion.37
  244.3 20.6 %gather_fusion.1 = bf16[4096,512]{1,0:T(8,128)(2,1)} fusion(bf16[5120,512]{1,0:T(8,128)(2,1)} %get-tuple-element.167, s32[4096]{0:T(1024)S(1)} %fusion.37), kind=kCustom, calls=%fused_computation.1.clone.clone.1 | custom fusion | bytes 8404992 | tf_op jit(solution)/shard_map/while/body/eval_jaxpr/gather | solution.py:77
  264.9 7.0 fusion.39
  271.8 18.1 %scatter_fusion.1 = f32[24,128,512]{2,1,0:T(8,128)} fusion(f32[24,128,512]{2,1,0:T(8,128)} %get-tuple-element.155, s32[32]{0:T(128)S(1)} %get-tuple-element.143, f32[32,128,512]{2,1,0:T(8,128)} %fusion.39), kind=kCustom, calls=%fused_computation.3.clone.clone.1 | custom fusion | flops 2097152 | bytes 25165952 | tf_op jit(solution)/shard_map/while/body/eval_jaxpr/scatter-add | solution.py:86
  289.9 20.6 %gather_fusion = bf16[4096,512]{1,0:T(8,128)(2,1)} fusion(bf16[5120,512]{1,0:T(8,128)(2,1)} %get-tuple-element.165, s32[4096]{0:T(1024)S(1)} %fusion.37), kind=kCustom, calls=%fused_computation.clone.clone.1 | custom fusion | bytes 8404992 | tf_op jit(solution)/shard_map/while/body/eval_jaxpr/gather | solution.py:76
  310.5 7.0 fusion.38
  317.5 18.1 %scatter_fusion = f32[24,512,128]{2,1,0:T(8,128)} fusion(f32[24,512,128]{2,1,0:T(8,128)} %get-tuple-element.154, s32[32]{0:T(128)S(1)} %get-tuple-element.143, f32[32,512,128]{2,1,0:T(8,128)} %fusion.38), kind=kCustom, calls=%fused_computation.2.clone.clone.1 | custom fusion | flops 2097152 | bytes 25165952 | tf_op jit(solution)/shard_map/while/body/eval_jaxpr/scatter-add | solution.py:86
  335.6 0.1 fusion.37
  335.7 20.6 %gather_fusion.1 = bf16[4096,512]{1,0:T(8,128)(2,1)} fusion(bf16[5120,512]{1,0:T(8,128)(2,1)} %get-tuple-element.167, s32[4096]{0:T(1024)S(1)} %fusion.37), kind=kCustom, calls=%fused_computation.1.clone.clone.1 | custom fusion | bytes 8404992 | tf_op jit(solution)/shard_map/while/body/eval_jaxpr/gather | solution.py:77
  356.3 7.0 fusion.39
  363.3 18.5 %scatter_fusion.1 = f32[24,128,512]{2,1,0:T(8,128)} fusion(f32[24,128,512]{2,1,0:T(8,128)} %get-tuple-element.155, s32[32]{0:T(128)S(1)} %get-tuple-element.143, f32[32,128,512]{2,1,0:T(8,128)} %fusion.39), kind=kCustom, calls=%fused_computation.3.clone.clone.1 | custom fusion | flops 2097152 | bytes 25165952 | tf_op jit(solution)/shard_map/while/body/eval_jaxpr/scatter-add | solution.py:86
  381.7 20.6 %gather_fusion = bf16[4096,512]{1,0:T(8,128)(2,1)} fusion(bf16[5120,512]{1,0:T(8,128)(2,1)} %get-tuple-element.165, s32[4096]{0:T(1024)S(1)} %fusion.37), kind=kCustom, calls=%fused_computation.clone.clone.1 | custom fusion | bytes 8404992 | tf_op jit(solution)/shard_map/while/body/eval_jaxpr/gather | solution.py:76
  402.3 7.0 fusion.38
  409.3 18.4 %scatter_fusion = f32[24,512,128]{2,1,0:T(8,128)} fusion(f32[24,512,128]{2,1,0:T(8,128)} %get-tuple-element.154, s32[32]{0:T(128)S(1)} %get-tuple-element.143, f32[32,512,128]{2,1,0:T(8,128)} %fusion.38), kind=kCustom, calls=%fused_computation.2.clone.clone.1 | custom fusion | flops 2097152 | bytes 25165952 | tf_op jit(solution)/shard_map/while/body/eval_jaxpr/scatter-add | solution.py:86
  427.7 0.1 fusion.37
  427.8 20.6 %gather_fusion.1 = bf16[4096,512]{1,0:T(8,128)(2,1)} fusion(bf16[5120,512]{1,0:T(8,128)(2,1)} %get-tuple-element.167, s32[4096]{0:T(1024)S(1)} %fusion.37), kind=kCustom, calls=%fused_computation.1.clone.clone.1 | custom fusion | bytes 8404992 | tf_op jit(solution)/shard_map/while/body/eval_jaxpr/gather | solution.py:77
  448.4 7.0 fusion.39
  455.4 18.1 %scatter_fusion.1 = f32[24,128,512]{2,1,0:T(8,128)} fusion(f32[24,128,512]{2,1,0:T(8,128)} %get-tuple-element.155, s32[32]{0:T(128)S(1)} %get-tuple-element.143, f32[32,128,512]{2,1,0:T(8,128)} %fusion.39), kind=kCustom, calls=%fused_computation.3.clone.clone.1 | custom fusion | flops 2097152 | bytes 25165952 | tf_op jit(solution)/shard_map/while/body/eval_jaxpr/scatter-add | solution.py:86
  473.5 20.6 %gather_fusion = bf16[4096,512]{1,0:T(8,128)(2,1)} fusion(bf16[5120,512]{1,0:T(8,128)(2,1)} %get-tuple-element.165, s32[4096]{0:T(1024)S(1)} %fusion.37), kind=kCustom, calls=%fused_computation.clone.clone.1 | custom fusion | bytes 8404992 | tf_op jit(solution)/shard_map/while/body/eval_jaxpr/gather | solution.py:76
  494.1 7.0 fusion.38
  501.1 18.2 %scatter_fusion = f32[24,512,128]{2,1,0:T(8,128)} fusion(f32[24,512,128]{2,1,0:T(8,128)} %get-tuple-element.154, s32[32]{0:T(128)S(1)} %get-tuple-element.143, f32[32,512,128]{2,1,0:T(8,128)} %fusion.38), kind=kCustom, calls=%fused_computation.2.clone.clone.1 | custom fusion | flops 2097152 | bytes 25165952 | tf_op jit(solution)/shard_map/while/body/eval_jaxpr/scatter-add | solution.py:86
  519.2 0.0 reduce-scatter.5.cloned.1.call-update
  519.3 0.2 reduce-scatter.3.cloned.1.call-start
  519.5 0.5 reduce-scatter.3.cloned.1.call-update
  520.0 66.1 %reduce-scatter.5.cloned.1.call-done = f32[24,128,128]{2,1,0:T(8,128)} async-done(((f32[24,128,512]{2,1,0:T(8,128)}), f32[24,128,128]{2,1,0:T(8,128)}) %reduce-scatter.5.cloned.1.call-update) | async-done | bytes 1572880 | tf_op jit(solution)/shard_map/reduce_scatter | solution.py:97
  586.1 3.5 copy.23
  589.6 7.7 all-to-all-start.3
  597.2 57.7 %reduce-scatter.3.cloned.1.call-done = f32[24,128,128]{2,1,0:T(8,128)} async-done(((f32[24,512,128]{2,1,0:T(8,128)}), f32[24,128,128]{2,1,0:T(8,128)}) %reduce-scatter.3.cloned.1.call-update) | async-done | bytes 1572880 | tf_op jit(solution)/shard_map/reduce_scatter | solution.py:96
  654.9 2.3 copy.22
  657.3 0.0 all-to-all-done.3
  657.3 47.2 %all_to_all.47 = f32[24,1,16,8,128]{4,0,3,1,2:T(8,128)S(1)} all-to-all(f32[24,1,16,8,128]{4,0,3,1,2:T(8,128)S(1)} %bitcast.71), channel_id=1, replica_groups=mesh['row'=4,'col'=16,'layer'=4] {'col'}, dimensions={2} | all-to-all | bytes 3145728 | tf_op jit(solution)/shard_map/all_to_all | solution.py:106
  704.5 27.5 %all_to_all.48 = f32[24,16,8,128]{3,0,2,1:T(8,128)S(1)} all-to-all(f32[24,16,8,128]{3,0,2,1:T(8,128)S(1)} %bitcast.70), channel_id=1, replica_groups=mesh['row'=4,'col'=16,'layer'=4] {'row','layer'}, dimensions={1} | all-to-all | bytes 3145728 | tf_op jit(solution)/shard_map/all_to_all | solution.py:110
  732.0 1.6 fusion.16
  733.5 129.3 %all-gather = f32[6144,24]{1,0:T(8,128)S(1)} all-gather(f32[24,24]{1,0:T(8,128)S(1)} %fusion.16), channel_id=2, replica_groups=mesh['row'=4,'col'=16,'layer'=4] {'row','col','layer'}, dimensions={0}, use_global_device_ids=true | all-gather | bytes 592128 | tf_op jit(solution)/shard_map/all_gather | solution.py:10
  862.8 0.9 reduce_sum.19
  (10 shorter events, 0.1 us)
Async XLA Ops:
  11.0 31.5 %all-to-all-start = ((s32[64,2,2]{1,2,0:T(2,128)}), s32[64,2,2]{1,2,0:T(2,128)S(1)}, u32[]{:S(2)}, u32[]{:S(2)}) async-start(s32[64,2,2]{1,2,0:T(2,128)} %copy.19), calls=%async_computation | async-start | bytes 131072 | tf_op jit(solution)/shard_map/all_to_all | solution.py:57
  42.4 103.9 %all-to-all-start.1 = ((bf16[128,128,128]{2,1,0:T(8,128)(2,1)}), bf16[128,128,128]{2,1,0:T(8,128)(2,1)}, u32[]{:S(2)}, u32[]{:S(2)}) async-start(bf16[128,128,128]{2,1,0:T(8,128)(2,1)} %scatter_fusion.2), calls=%async_computation.1 | async-start | bytes 8388608 | tf_op jit(solution)/shard_map/all_to_all | solution.py:50
  52.9 533.3 %reduce-scatter.5.cloned.1.call-start = ((), (), s32[]{:S(2)}) async-start(), calls=%async_computation.8 | async-start | bytes 7864320 | tf_op jit(solution)/shard_map/reduce_scatter | solution.py:97
  519.3 135.7 %reduce-scatter.3.cloned.1.call-start = ((), (), s32[]{:S(2)}) async-start(), calls=%async_computation.7 | async-start | bytes 7864320 | tf_op jit(solution)/shard_map/reduce_scatter | solution.py:96
  589.6 67.7 %all-to-all-start.3 = ((f32[24,1,16,8,128]{4,0,3,1,2:T(8,128)}), f32[24,1,16,8,128]{4,0,3,1,2:T(8,128)S(1)}, u32[]{:S(2)}, u32[]{:S(2)}) async-start(f32[24,1,16,8,128]{4,0,3,1,2:T(8,128)} %bitcast.6), calls=%async_computation.5 | async-start | bytes 3145728 | tf_op jit(solution)/shard_map/all_to_all | solution.py:107
Sparse Core Ops, SparseCore 0:
  519.4 66.6 reduce-scatter.4
  588.7 66.2 reduce-scatter.2
